TPU v7x, 256 devices: a whole 4x4x8 slice. The times are simulated.
256 devices in a mesh: pix: 16 (over y_lo, x, core), ion: 16 (over y_hi, z).
Axes of the slice: x: 4, y: 4 (y_hi: 2, y_lo: 2; y = y_hi * 2 + y_lo), z: 8, core: 2. Of those that a mesh axis runs over, the one named last changes fastest.
Arguments:
- images: bfloat16 [20480, 32768], P('ion', 'pix')
- stencil: float32 [5, 32768], P(None, 'pix'), may hold values from 0.05 to 0.4
- pairs: int32 [768, 2], P('ion'), may hold values from 0 to 159, as said below
- live: int32 [16], P('ion'), may hold values from 16 to 48, as said below
- rule_of_block: int32 [160], replicated, may hold values from 0 to 63
- adduct: bfloat16 [64, 128, 128], P('ion'), may hold values from -6 to 6
Outputs:
- smoothed: bfloat16 [20480, 32768], P('ion', 'pix')
- scores: bfloat16 [768, 128, 128], P('ion', 'pix')
Inputs may be any that keep to these rules, and one draw needn't show every extreme that they name: Slot s belongs to ion block range of index s // 48 of ion: a lies in that index's own 20480 // (128 * 16) blocks, and |a - b| <= 3. Entries of unused slots are valid pairs too. `live`: some index of ion uses all its slots.
All inputs are finite; a program needn't handle non-finite values.
Results may differ from a plain program's by a relative error of at most 0.0053.
Values may be sent and summed in bfloat16 or wider, within the bound.
A program may use at most 192 MiB of HBM per device.

v0:
```python
import jax
import jax.numpy as jnp
from jax import lax
from jax.sharding import PartitionSpec as P

REACH = 3
slot_group = 16


def extended_2(array, sides, width):
    for axis, dim in sides:
        size, length = (lax.axis_size(axis), array.shape[dim])
        up = [(i, (i + 1) % size) for i in range(size - 1)]
        down = [(j, i) for i, j in up]
        last = lax.slice_in_dim(array, length - width, length, axis=dim)
        first = lax.slice_in_dim(array, 0, width, axis=dim)
        before = lax.ppermute(last, axis, up)
        after = lax.ppermute(first, axis, down)
        array = jnp.concatenate([before, array, after], axis=dim)
    return array


def on_device(images, stencil, pairs, live, rule_of_block, adduct):
    local_rows, pix_local = images.shape
    block = adduct.shape[1]
    local_blocks = local_rows // block
    padded = extended_2(images, (("pix", 1),), 2)
    total = jnp.zeros((local_rows, pix_local), jnp.float32)
    for tap in range(5):
        total = total + stencil[tap][None, :] * padded[:, tap : tap + pix_local].astype(jnp.float32)
    smoothed = total.astype(jnp.bfloat16)
    extended = extended_2(smoothed, (("ion", 0),), REACH * block)
    values = extended.astype(jnp.float32)
    squares = jnp.sum(values * values, axis=1)
    pixel_count = pix_local * lax.axis_size("pix")
    energy = lax.psum(squares, "pix") / pixel_count
    inverse = 1.0 / jnp.sqrt(energy + 1e-06)
    lookup_tables = lax.all_gather(adduct, "ion", axis=0, tiled=True)
    first = lax.axis_index("ion") * local_blocks
    ext_blocks = extended.reshape(local_blocks + 2 * REACH, block, pix_local)
    inv_blocks = inverse.reshape(local_blocks + 2 * REACH, block)
    slots = pairs.shape[0]
    relative = pairs - first + REACH

    def group_gram(start):
        chosen = lax.dynamic_slice_in_dim(relative, start, slot_group, 0)
        left_operand = jnp.take(ext_blocks, chosen[:, 0], axis=0)
        right_operand = jnp.take(ext_blocks, chosen[:, 1], axis=0)
        return jnp.einsum(
            "uwf,uvf->uwv", left_operand, right_operand, preferred_element_type=jnp.float32
        )

    grams = jnp.concatenate(
        [group_gram(step * slot_group) for step in range(slots // slot_group)], axis=0
    )
    inv_left = jnp.take(inv_blocks, relative[:, 0], axis=0)
    inv_right = jnp.take(inv_blocks, relative[:, 1], axis=0)
    rules = jnp.take(rule_of_block, pairs[:, 1], axis=0)
    matrices = jnp.take(lookup_tables, rules, axis=0)
    share = block // lax.axis_size("pix")
    offset = lax.axis_index("pix") * share
    gram = lax.psum(grams, "pix")
    coloc = (gram * inv_left[:, :, None] * inv_right[:, None, :] / pixel_count).astype(jnp.bfloat16)
    complete_scores = jnp.einsum(
        "src,scd->srd", coloc, matrices, preferred_element_type=jnp.float32
    )
    scores = lax.dynamic_slice_in_dim(complete_scores, offset, share, 1)
    used = jnp.arange(slots, dtype=jnp.int32) < live[0]
    scores = jnp.where(used[:, None, None], scores, 0.0).astype(jnp.bfloat16)
    return (smoothed, scores)


def solution(mesh):
    return jax.shard_map(
        on_device,
        mesh=mesh,
        in_specs=(
            P("ion", "pix"),
            P(None, "pix"),
            P("ion", None),
            P("ion"),
            P(),
            P("ion", None, None),
        ),
        out_specs=(P("ion", "pix"), P("ion", "pix", None)),
        check_vma=False,
    )
```

profile of v0, /device:TPU:7, one launch (start us, length us, event | category | flops | bytes accessed | tf_op | source)
XLA Modules:
  0.0 307.4 jit_solution(16997683368433207593)
XLA Ops:
  8.1 1.3 fusion.33
  9.4 2.6 collective-permute-start.1
  12.0 5.4 %collective-permute-start = (bf16[1280,2]{1,0:T(8,128)(2,1)S(1)}, bf16[1280,2]{1,0:T(8,128)(2,1)S(1)}, u32[]{:S(2)}, u32[]{:S(2)}) collective-permute-start(bf16[1280,2]{1,0:T(8,128)(2,1)S(1)} %get-tuple-element.27), channel_id=1, source_target_pairs={{0,16},{16,32},{32,48},{48,64},{64,80},{80,96},{96,112},{112,128},... | collective-permute-start | bytes 15368 | tf_op jit(solution)/shard_map/ppermute | solution.py:17
  17.4 3.0 constant_dynamic-update-slice_fusion.1
  21.4 8.8 %add_convert_fusion = bf16[1280,2048]{1,0:T(8,128)(2,1)S(1)} fusion(bf16[1280,2048]{1,0:T(8,128)(2,1)S(1)} %bitcast.51, bf16[1280,2]{1,0:T(8,128)(2,1)S(1)} %collective-permute-done, bf16[1280,2050]{1,0:T(8,128)(2,1)S(1)} %constant_dynamic-update-slice_fusion, f32[2048]{0:T(1024)S(1)} %bitcast.55, f32[2048]{0:T(1024)S(1)} %bitcast.56, f32[2048]{0:T(1024)S(1)} %bitcast.53, ...), kind=kLoop, calls=%fused_computation.11 | loop fusion | flops 55050240 | bytes 21017600 | tf_op jit(solution)/shard_map/convert_element_type | solution.py:31
  30.2 2.3 copy-done.1
  33.0 4.7 %collective-permute-start.2 = (bf16[384,2048]{1,0:T(8,128)(2,1)S(1)}, bf16[384,2048]{1,0:T(8,128)(2,1)}, u32[]{:S(2)}, u32[]{:S(2)}) collective-permute-start(bf16[384,2048]{1,0:T(8,128)(2,1)S(1)} %get-tuple-element.24), channel_id=1, source_target_pairs={{0,1},{1,2},{2,3},{3,4},{4,5},{5,6},{6,7},{7,8},{8,9},{9,10},{10,1... | collective-permute-start | bytes 4718600 | tf_op jit(solution)/shard_map/ppermute | solution.py:17
  39.4 33.0 %collective-permute-done.2 = bf16[384,2048]{1,0:T(8,128)(2,1)} collective-permute-done((bf16[384,2048]{1,0:T(8,128)(2,1)S(1)}, bf16[384,2048]{1,0:T(8,128)(2,1)}, u32[]{:S(2)}, u32[]{:S(2)}) %collective-permute-start.2) | collective-permute-done | bytes 1572896 | tf_op jit(solution)/shard_map/ppermute | solution.py:17
  72.4 5.8 %collective-permute-done.3 = bf16[384,2048]{1,0:T(8,128)(2,1)} collective-permute-done((bf16[384,2048]{1,0:T(8,128)(2,1)S(1)}, bf16[384,2048]{1,0:T(8,128)(2,1)}, u32[]{:S(2)}, u32[]{:S(2)}) %collective-permute-start.3) | collective-permute-done | bytes 1572896 | tf_op jit(solution)/shard_map/ppermute | solution.py:18
  78.1 7.5 %multiply_reduce_fusion = (f32[2048]{0:T(1024)S(1)}, bf16[2048,2048]{1,0:T(8,128)(2,1)}) fusion(bf16[384,2048]{1,0:T(8,128)(2,1)} %collective-permute-done.3, bf16[1280,2048]{1,0:T(8,128)(2,1)} %copy-done.1, bf16[384,2048]{1,0:T(8,128)(2,1)} %collective-permute-done.2), kind=kLoop, calls=%fused_computation.10 | loop fusion | flops 37746688 | bytes 16785408 | tf_op jit(solution)/shard_map/reduce_sum | solution.py:34
  85.6 8.2 %gather_fusion.2 = bf16[16,128,2048]{2,1,0:T(8,128)(2,1)} fusion(bf16[16,128,2048]{2,1,0:T(8,128)(2,1)} %bitcast.44, s32[1024]{0:T(1024)S(1)} %get-tuple-element.50), kind=kCustom, calls=%fused_computation.clone | custom fusion | bytes 16777280 | tf_op jit(solution)/shard_map/jit(_take)/gather | solution.py:47
  93.8 8.1 %gather_fusion.3 = bf16[16,128,2048]{2,1,0:T(8,128)(2,1)} fusion(bf16[16,128,2048]{2,1,0:T(8,128)(2,1)} %bitcast.45, s32[1024]{0:T(1024)S(1)} %get-tuple-element.49), kind=kCustom, calls=%fused_computation.2.clone | custom fusion | bytes 16777280 | tf_op jit(solution)/shard_map/jit(_take)/gather | solution.py:48
  102.0 8.3 %gather_fusion.4 = bf16[16,128,2048]{2,1,0:T(8,128)(2,1)} fusion(bf16[16,128,2048]{2,1,0:T(8,128)(2,1)} %bitcast.46, s32[1024]{0:T(1024)S(1)} %get-tuple-element.48), kind=kCustom, calls=%fused_computation.3.clone | custom fusion | bytes 16777280 | tf_op jit(solution)/shard_map/jit(_take)/gather | solution.py:47
  110.2 8.2 %gather_fusion.5 = bf16[16,128,2048]{2,1,0:T(8,128)(2,1)} fusion(bf16[16,128,2048]{2,1,0:T(8,128)(2,1)} %bitcast.47, s32[1024]{0:T(1024)S(1)} %get-tuple-element.47), kind=kCustom, calls=%fused_computation.4.clone | custom fusion | bytes 16777280 | tf_op jit(solution)/shard_map/jit(_take)/gather | solution.py:48
  118.4 8.2 %gather_fusion.6 = bf16[16,128,2048]{2,1,0:T(8,128)(2,1)} fusion(bf16[16,128,2048]{2,1,0:T(8,128)(2,1)} %bitcast.48, s32[1024]{0:T(1024)S(1)} %get-tuple-element.46), kind=kCustom, calls=%fused_computation.5.clone | custom fusion | bytes 16777280 | tf_op jit(solution)/shard_map/jit(_take)/gather | solution.py:47
  126.6 8.2 %gather_fusion.7 = bf16[16,128,2048]{2,1,0:T(8,128)(2,1)} fusion(bf16[16,128,2048]{2,1,0:T(8,128)(2,1)} %bitcast.49, s32[1024]{0:T(1024)S(1)} %get-tuple-element.45), kind=kCustom, calls=%fused_computation.6.clone | custom fusion | bytes 16777280 | tf_op jit(solution)/shard_map/jit(_take)/gather | solution.py:48
  134.8 8.4 %fusion.6 = f32[16,128,128]{2,1,0:T(8,128)S(1)} fusion(bf16[16,128,2048]{2,1,0:T(8,128)(2,1)} %gather_fusion.3, bf16[16,128,2048]{2,1,0:T(8,128)(2,1)} %gather_fusion.2, pred[16]{0:T(512)(128)(4,1)S(1)} %get-tuple-element.43, pred[16]{0:T(512)(128)(4,1)S(1)} %get-tuple-element.12), kind=kOutput, calls=%fused_computation.19 | convolution fusion | flops 1082130432 | bytes 17825824 | tf_op jit(solution)/shard_map/uwf,uvf->uwv/dot_general | solution.py:49
  143.2 8.4 %fusion.3 = f32[16,128,128]{2,1,0:T(8,128)S(1)} fusion(bf16[16,128,2048]{2,1,0:T(8,128)(2,1)} %gather_fusion.5, bf16[16,128,2048]{2,1,0:T(8,128)(2,1)} %gather_fusion.4, pred[16]{0:T(512)(128)(4,1)S(1)} %get-tuple-element.39, pred[16]{0:T(512)(128)(4,1)S(1)} %get-tuple-element.41), kind=kOutput, calls=%fused_computation.16 | convolution fusion | flops 1082130432 | bytes 17825824 | tf_op jit(solution)/shard_map/uwf,uvf->uwv/dot_general | solution.py:49
  151.6 8.4 %fusion = f32[16,128,128]{2,1,0:T(8,128)S(1)} fusion(bf16[16,128,2048]{2,1,0:T(8,128)(2,1)} %gather_fusion.7, bf16[16,128,2048]{2,1,0:T(8,128)(2,1)} %gather_fusion.6, pred[16]{0:T(512)(128)(4,1)S(1)} %get-tuple-element.35, pred[16]{0:T(512)(128)(4,1)S(1)} %get-tuple-element.37), kind=kOutput, calls=%fused_computation.13 | convolution fusion | flops 1082130432 | bytes 17825824 | tf_op jit(solution)/shard_map/uwf,uvf->uwv/dot_general | solution.py:49
  160.0 2.0 pad_maximum_fusion.2
  163.6 27.1 %psum.15 = f32[2048]{0:T(1024)S(1)} all-reduce(f32[2048]{0:T(1024)S(1)} %get-tuple-element.10), channel_id=1, replica_groups=mesh['pix'=16,'ion'=16] {'pix'}, use_global_device_ids=true, to_apply=%region_2.0 | all-reduce | flops 2048 | bytes 16384 | tf_op jit(solution)/shard_map/psum | solution.py:36
  192.0 2.4 gather_fusion.1
  194.5 101.7 %all-reduce.2.cloned.1.call-done = f32[48,128,128]{2,1,0:T(8,128)} async-done(((f32[48,128,128]{2,1,0:T(8,128)}), f32[48,128,128]{2,1,0:T(8,128)}) %all-reduce.2.cloned.1.call-update) | async-done | bytes 3145744 | tf_op jit(solution)/shard_map/psum | solution.py:62
  296.2 3.0 fusion.19
  (42 shorter events, 6.0 us)
Async XLA Ops:
  8.0 154.7 %copy-start = (s32[160]{0:T(256)S(1)}, s32[160]{0:T(256)}, u32[]{:S(2)}) copy-start(s32[160]{0:T(256)} %param.14) | copy-start | bytes 1924
  8.0 13.4 %slice-start = ((s8[5242880]{0:T(1024)(128)(4,1)}), s8[1048576]{0:T(1024)(128)(4,1)S(1)}, s32[]{:S(2)}) async-start(s8[5242880]{0:T(1024)(128)(4,1)} %bitcast.50), calls=%async_computation.2 | async-start | bytes 2097152
  8.0 12.4 %copy-start.2 = (f32[5,2048]{1,0:T(8,128)S(1)}, f32[5,2048]{1,0:T(8,128)}, u32[]{:S(2)}) copy-start(f32[5,2048]{1,0:T(8,128)} %param.11) | copy-start | bytes 122884
  8.0 184.0 %all-gather.2.cloned.1.call-start = ((), (), s32[]{:S(2)}) async-start(), calls=%async_computation.1 | async-start | bytes 2228224 | tf_op jit(solution)/shard_map/all_gather | solution.py:38
  9.4 11.0 %collective-permute-start.1 = (bf16[1280,2]{1,0:T(8,128)(2,1)S(1)}, bf16[1280,2]{1,0:T(8,128)(2,1)S(1)}, u32[]{:S(2)}, u32[]{:S(2)}) collective-permute-start(bf16[1280,2]{1,0:T(8,128)(2,1)S(1)} %get-tuple-element.26), channel_id=1, source_target_pairs={{16,0},{32,16},{48,32},{64,48},{80,64},{96,80},{112,96},{128,112},... | collective-permute-start | bytes 15368 | tf_op jit(solution)/shard_map/ppermute | solution.py:18
  12.0 9.4 %slice-start.1 = ((s8[5242880]{0:T(1024)(128)(4,1)}), s8[4194304]{0:T(1024)(128)(4,1)S(1)}, s32[]{:S(2)}) async-start(s8[5242880]{0:T(1024)(128)(4,1)} %bitcast.50), calls=%async_computation.3 | async-start | bytes 8388608
  12.0 9.4 %collective-permute-start = (bf16[1280,2]{1,0:T(8,128)(2,1)S(1)}, bf16[1280,2]{1,0:T(8,128)(2,1)S(1)}, u32[]{:S(2)}, u32[]{:S(2)}) collective-permute-start(bf16[1280,2]{1,0:T(8,128)(2,1)S(1)} %get-tuple-element.27), channel_id=1, source_target_pairs={{0,16},{16,32},{32,48},{48,64},{64,80},{80,96},{96,112},{112,128},... | collective-permute-start | bytes 15368 | tf_op jit(solution)/shard_map/ppermute | solution.py:17
  21.4 17.9 %copy-start.3 = (s32[48,2]{0,1:T(2,128)S(1)}, s32[48,2]{0,1:T(2,128)}, u32[]{:S(2)}) copy-start(s32[48,2]{0,1:T(2,128)} %param.12) | copy-start | bytes 1156
  30.2 2.4 copy-start.1
  33.0 39.4 %collective-permute-start.2 = (bf16[384,2048]{1,0:T(8,128)(2,1)S(1)}, bf16[384,2048]{1,0:T(8,128)(2,1)}, u32[]{:S(2)}, u32[]{:S(2)}) collective-permute-start(bf16[384,2048]{1,0:T(8,128)(2,1)S(1)} %get-tuple-element.24), channel_id=1, source_target_pairs={{0,1},{1,2},{2,3},{3,4},{4,5},{5,6},{6,7},{7,8},{8,9},{9,10},{10,1... | collective-permute-start | bytes 4718600 | tf_op jit(solution)/shard_map/ppermute | solution.py:17
  37.7 40.5 %collective-permute-start.3 = (bf16[384,2048]{1,0:T(8,128)(2,1)S(1)}, bf16[384,2048]{1,0:T(8,128)(2,1)}, u32[]{:S(2)}, u32[]{:S(2)}) collective-permute-start(bf16[384,2048]{1,0:T(8,128)(2,1)S(1)} %get-tuple-element.25), channel_id=1, source_target_pairs={{1,0},{2,1},{3,2},{4,3},{5,4},{6,5},{7,6},{8,7},{9,8},{10,9},{11,1... | collective-permute-start | bytes 4718600 | tf_op jit(solution)/shard_map/ppermute | solution.py:18
  39.0 257.2 %all-reduce.2.cloned.1.call-start = ((), (), s32[]{:S(2)}) async-start(), calls=%async_computation | async-start | bytes 6291456 | tf_op jit(solution)/shard_map/psum | solution.py:62
Sparse Core Ops, SparseCore 0:
  39.1 102.5 all-gather.1
Sparse Core Ops, SparseCore 1:
  162.1 134.0 all-reduce.1
where the time goes:
time: 308 us; the launch traced here: 307 us
  waiting for transfers between devices  141 us (46%)
  local copies, waits for them, and re-layouts  60.8 us (20%)
  matrix products  28.1 us (9%)
  blocking collectives  27.1 us (9%)
  other arithmetic  19.4 us (6%)
  between operations  16.4 us (5%)
  starting transfers between devices  14.2 us (5%)
    psum x1, waiting for transfers between devices, on_device(): gram = lax.psum(grams, 'pix')  102 us
    ppermute x2, waiting for transfers between devices, extended_2(): before = lax.ppermute(last, axis, up)  33.8 us
    psum x1, blocking collectives, on_device(): energy = lax.psum(squares, 'pix') / pixel_count  27.1 us
    dot_general x3, matrix products, group_gram(): jnp.einsum('uwf,uvf->uwv', left_operand, right_operand, preferred_element...  25.1 us
    gather x3, local copies, waits for them, and re-layouts, group_gram(): left_operand = jnp.take(ext_blocks, chosen[:, 0], axis=0)  24.7 us
    gather x3, local copies, waits for them, and re-layouts, group_gram(): right_operand = jnp.take(ext_blocks, chosen[:, 1], axis=0)  24.5 us
    ppermute x2, starting transfers between devices, extended_2(): before = lax.ppermute(last, axis, up)  10.1 us
    convert_element_type x1, other arithmetic, on_device(): smoothed = total.astype(jnp.bfloat16)  8.82 us
  transfers between devices with their start and end apart: 6, of which 4 were waited for; matrix products, arithmetic and copies ran while one was open for 30% of the time, Pallas kernels for 0%

commit v1 on v0

--- a/solution.py
+++ b/solution.py
@@ -59,7 +59,7 @@
     matrices = jnp.take(lookup_tables, rules, axis=0)
     share = block // lax.axis_size("pix")
     offset = lax.axis_index("pix") * share
-    gram = lax.psum(grams, "pix")
+    gram = jnp.sum(lax.all_gather(grams, "pix"), axis=0)
     coloc = (gram * inv_left[:, :, None] * inv_right[:, None, :] / pixel_count).astype(jnp.bfloat16)
     complete_scores = jnp.einsum(
         "src,scd->srd", coloc, matrices, preferred_element_type=jnp.float32

time: 308 us -> 446 us (1.45)
  waiting for transfers between devices: 141 us -> 261 us
  other arithmetic: 19.4 us -> 36.6 us
    all_gather x0 -> x1, waiting for transfers between devices: none -> 221 us  [on_device(): gram = jnp.sum(lax.all_gather(grams, 'pix'), axis=0)]
    psum x1 -> x0, waiting for transfers between devices: 102 us -> none  [on_device(): gram = lax.psum(grams, 'pix')]
    reduce_sum x0 -> x1, other arithmetic: none -> 17.3 us  [on_device(): gram = jnp.sum(lax.all_gather(grams, 'pix'), axis=0)]
  transfers between devices with their start and end apart: 6 -> 6, of which waited for: 4 -> 4; matrix products, arithmetic and copies ran while one was open for 30% -> 21% of each run, Pallas kernels for 0% -> 0%
where the time goes in v1:
time: 446 us; the launch traced here: 444 us
  waiting for transfers between devices  261 us (59%)
  local copies, waits for them, and re-layouts  62 us (14%)
  other arithmetic  36.6 us (8%)
  matrix products  27.6 us (6%)
  blocking collectives  27.5 us (6%)
  between operations  15 us (3%)
  starting transfers between devices  14.2 us (3%)
    all_gather x1, waiting for transfers between devices, on_device(): gram = jnp.sum(lax.all_gather(grams, 'pix'), axis=0)  221 us
    ppermute x2, waiting for transfers between devices, extended_2(): before = lax.ppermute(last, axis, up)  33.8 us
    psum x1, blocking collectives, on_device(): energy = lax.psum(squares, 'pix') / pixel_count  27.5 us
    dot_general x3, matrix products, group_gram(): jnp.einsum('uwf,uvf->uwv', left_operand, right_operand, preferred_element...  25.2 us
    gather x3, local copies, waits for them, and re-layouts, group_gram(): left_operand = jnp.take(ext_blocks, chosen[:, 0], axis=0)  24.7 us
    gather x3, local copies, waits for them, and re-layouts, group_gram(): right_operand = jnp.take(ext_blocks, chosen[:, 1], axis=0)  24.5 us
    reduce_sum x1, other arithmetic, on_device(): gram = jnp.sum(lax.all_gather(grams, 'pix'), axis=0)  17.3 us
    ppermute x2, starting transfers between devices, extended_2(): before = lax.ppermute(last, axis, up)  10.1 us
  transfers between devices with their start and end apart: 6, of which 4 were waited for; matrix products, arithmetic and copies ran while one was open for 21% of the time, Pallas kernels for 0%

profile of v1, /device:TPU:7, one launch (start us, length us, event | category | flops | bytes accessed | tf_op | source)
XLA Modules:
  0.0 443.6 jit_solution(4695164438002046226)
XLA Ops:
  8.6 2.6 collective-permute-start.1
  11.2 5.4 %collective-permute-start = (bf16[1280,2]{1,0:T(8,128)(2,1)S(1)}, bf16[1280,2]{1,0:T(8,128)(2,1)S(1)}, u32[]{:S(2)}, u32[]{:S(2)}) collective-permute-start(bf16[1280,2]{1,0:T(8,128)(2,1)S(1)} %get-tuple-element.27), channel_id=1, source_target_pairs={{0,16},{16,32},{32,48},{48,64},{64,80},{80,96},{96,112},{112,128},... | collective-permute-start | bytes 15368 | tf_op jit(solution)/shard_map/ppermute | solution.py:17
  16.5 3.0 constant_dynamic-update-slice_fusion.1
  20.5 8.8 %add_convert_fusion = bf16[1280,2048]{1,0:T(8,128)(2,1)S(1)} fusion(bf16[1280,2048]{1,0:T(8,128)(2,1)S(1)} %bitcast.53, bf16[1280,2]{1,0:T(8,128)(2,1)S(1)} %collective-permute-done, bf16[1280,2050]{1,0:T(8,128)(2,1)S(1)} %constant_dynamic-update-slice_fusion, f32[2048]{0:T(1024)S(1)} %bitcast.57, f32[2048]{0:T(1024)S(1)} %bitcast.58, f32[2048]{0:T(1024)S(1)} %bitcast.55, ...), kind=kLoop, calls=%fused_computation.11 | loop fusion | flops 55050240 | bytes 21017600 | tf_op jit(solution)/shard_map/convert_element_type | solution.py:31
  29.4 2.3 copy-done.1
  32.1 4.7 %collective-permute-start.2 = (bf16[384,2048]{1,0:T(8,128)(2,1)S(1)}, bf16[384,2048]{1,0:T(8,128)(2,1)}, u32[]{:S(2)}, u32[]{:S(2)}) collective-permute-start(bf16[384,2048]{1,0:T(8,128)(2,1)S(1)} %get-tuple-element.24), channel_id=1, source_target_pairs={{0,1},{1,2},{2,3},{3,4},{4,5},{5,6},{6,7},{7,8},{8,9},{9,10},{10,1... | collective-permute-start | bytes 4718600 | tf_op jit(solution)/shard_map/ppermute | solution.py:17
  38.5 33.0 %collective-permute-done.2 = bf16[384,2048]{1,0:T(8,128)(2,1)} collective-permute-done((bf16[384,2048]{1,0:T(8,128)(2,1)S(1)}, bf16[384,2048]{1,0:T(8,128)(2,1)}, u32[]{:S(2)}, u32[]{:S(2)}) %collective-permute-start.2) | collective-permute-done | bytes 1572896 | tf_op jit(solution)/shard_map/ppermute | solution.py:17
  71.5 5.8 %collective-permute-done.3 = bf16[384,2048]{1,0:T(8,128)(2,1)} collective-permute-done((bf16[384,2048]{1,0:T(8,128)(2,1)S(1)}, bf16[384,2048]{1,0:T(8,128)(2,1)}, u32[]{:S(2)}, u32[]{:S(2)}) %collective-permute-start.3) | collective-permute-done | bytes 1572896 | tf_op jit(solution)/shard_map/ppermute | solution.py:18
  77.3 7.5 %multiply_reduce_fusion = (f32[2048]{0:T(1024)S(1)}, bf16[2048,2048]{1,0:T(8,128)(2,1)}) fusion(bf16[384,2048]{1,0:T(8,128)(2,1)} %collective-permute-done.3, bf16[1280,2048]{1,0:T(8,128)(2,1)} %copy-done.1, bf16[384,2048]{1,0:T(8,128)(2,1)} %collective-permute-done.2), kind=kLoop, calls=%fused_computation.10 | loop fusion | flops 37746688 | bytes 16785408 | tf_op jit(solution)/shard_map/reduce_sum | solution.py:34
  84.8 8.2 %gather_fusion.2 = bf16[16,128,2048]{2,1,0:T(8,128)(2,1)} fusion(bf16[16,128,2048]{2,1,0:T(8,128)(2,1)} %bitcast.45, s32[1024]{0:T(1024)S(1)} %get-tuple-element.50), kind=kCustom, calls=%fused_computation.clone | custom fusion | bytes 16777280 | tf_op jit(solution)/shard_map/jit(_take)/gather | solution.py:47
  93.0 8.1 %gather_fusion.3 = bf16[16,128,2048]{2,1,0:T(8,128)(2,1)} fusion(bf16[16,128,2048]{2,1,0:T(8,128)(2,1)} %bitcast.46, s32[1024]{0:T(1024)S(1)} %get-tuple-element.49), kind=kCustom, calls=%fused_computation.2.clone | custom fusion | bytes 16777280 | tf_op jit(solution)/shard_map/jit(_take)/gather | solution.py:48
  101.1 8.3 %gather_fusion.4 = bf16[16,128,2048]{2,1,0:T(8,128)(2,1)} fusion(bf16[16,128,2048]{2,1,0:T(8,128)(2,1)} %bitcast.47, s32[1024]{0:T(1024)S(1)} %get-tuple-element.48), kind=kCustom, calls=%fused_computation.3.clone | custom fusion | bytes 16777280 | tf_op jit(solution)/shard_map/jit(_take)/gather | solution.py:47
  109.4 8.2 %gather_fusion.5 = bf16[16,128,2048]{2,1,0:T(8,128)(2,1)} fusion(bf16[16,128,2048]{2,1,0:T(8,128)(2,1)} %bitcast.48, s32[1024]{0:T(1024)S(1)} %get-tuple-element.47), kind=kCustom, calls=%fused_computation.4.clone | custom fusion | bytes 16777280 | tf_op jit(solution)/shard_map/jit(_take)/gather | solution.py:48
  117.6 8.2 %gather_fusion.6 = bf16[16,128,2048]{2,1,0:T(8,128)(2,1)} fusion(bf16[16,128,2048]{2,1,0:T(8,128)(2,1)} %bitcast.49, s32[1024]{0:T(1024)S(1)} %get-tuple-element.46), kind=kCustom, calls=%fused_computation.5.clone | custom fusion | bytes 16777280 | tf_op jit(solution)/shard_map/jit(_take)/gather | solution.py:47
  125.8 8.2 %gather_fusion.7 = bf16[16,128,2048]{2,1,0:T(8,128)(2,1)} fusion(bf16[16,128,2048]{2,1,0:T(8,128)(2,1)} %bitcast.50, s32[1024]{0:T(1024)S(1)} %get-tuple-element.45), kind=kCustom, calls=%fused_computation.6.clone | custom fusion | bytes 16777280 | tf_op jit(solution)/shard_map/jit(_take)/gather | solution.py:48
  134.0 8.4 %fusion.6 = f32[16,128,128]{2,1,0:T(8,128)S(1)} fusion(bf16[16,128,2048]{2,1,0:T(8,128)(2,1)} %gather_fusion.3, bf16[16,128,2048]{2,1,0:T(8,128)(2,1)} %gather_fusion.2, pred[16]{0:T(512)(128)(4,1)S(1)} %get-tuple-element.43, pred[16]{0:T(512)(128)(4,1)S(1)} %get-tuple-element.12), kind=kOutput, calls=%fused_computation.19 | convolution fusion | flops 1082130432 | bytes 17825824 | tf_op jit(solution)/shard_map/uwf,uvf->uwv/dot_general | solution.py:49
  142.4 8.4 %fusion.3 = f32[16,128,128]{2,1,0:T(8,128)S(1)} fusion(bf16[16,128,2048]{2,1,0:T(8,128)(2,1)} %gather_fusion.5, bf16[16,128,2048]{2,1,0:T(8,128)(2,1)} %gather_fusion.4, pred[16]{0:T(512)(128)(4,1)S(1)} %get-tuple-element.39, pred[16]{0:T(512)(128)(4,1)S(1)} %get-tuple-element.41), kind=kOutput, calls=%fused_computation.16 | convolution fusion | flops 1082130432 | bytes 17825824 | tf_op jit(solution)/shard_map/uwf,uvf->uwv/dot_general | solution.py:49
  150.8 8.4 %fusion = f32[16,128,128]{2,1,0:T(8,128)S(1)} fusion(bf16[16,128,2048]{2,1,0:T(8,128)(2,1)} %gather_fusion.7, bf16[16,128,2048]{2,1,0:T(8,128)(2,1)} %gather_fusion.6, pred[16]{0:T(512)(128)(4,1)S(1)} %get-tuple-element.35, pred[16]{0:T(512)(128)(4,1)S(1)} %get-tuple-element.37), kind=kOutput, calls=%fused_computation.13 | convolution fusion | flops 1082130432 | bytes 17825824 | tf_op jit(solution)/shard_map/uwf,uvf->uwv/dot_general | solution.py:49
  159.2 2.0 pad_maximum_fusion.2
  162.7 27.5 %psum.7 = f32[2048]{0:T(1024)S(1)} all-reduce(f32[2048]{0:T(1024)S(1)} %get-tuple-element.10), channel_id=1, replica_groups=mesh['pix'=16,'ion'=16] {'pix'}, use_global_device_ids=true, to_apply=%region_2.0 | all-reduce | flops 2048 | bytes 16384 | tf_op jit(solution)/shard_map/psum | solution.py:36
  191.6 3.6 gather_fusion.1
  195.2 221.1 %all-gather.6.cloned.1.call-done = f32[768,128,128]{2,1,0:T(8,128)} async-done(((f32[48,128,128]{2,1,0:T(8,128)}), f32[768,128,128]{2,1,0:T(8,128)}) %all-gather.6.cloned.1.call-update) | async-done | bytes 50331664 | tf_op jit(solution)/shard_map/all_gather | solution.py:62
  416.3 17.3 %reduce_sum.18 = f32[48,128,128]{2,1,0:T(8,128)S(1)} reduce(f32[16,48,128,128]{3,2,1,0:T(8,128)} %bitcast.51, f32[]{:T(128)} %constant.40.clone.1), dimensions={0}, to_apply=%region_0.2 | reduce | flops 11796480 | bytes 53477380 | tf_op jit(solution)/shard_map/reduce_sum | solution.py:62
  433.5 2.5 fusion.19
  (43 shorter events, 7.3 us)
Async XLA Ops:
  7.2 154.7 %copy-start = (s32[160]{0:T(256)S(1)}, s32[160]{0:T(256)}, u32[]{:S(2)}) copy-start(s32[160]{0:T(256)} %param.14) | copy-start | bytes 1924
  7.2 13.4 %slice-start = ((s8[5242880]{0:T(1024)(128)(4,1)}), s8[1048576]{0:T(1024)(128)(4,1)S(1)}, s32[]{:S(2)}) async-start(s8[5242880]{0:T(1024)(128)(4,1)} %bitcast.52), calls=%async_computation.2 | async-start | bytes 2097152
  7.2 12.4 %copy-start.2 = (f32[5,2048]{1,0:T(8,128)S(1)}, f32[5,2048]{1,0:T(8,128)}, u32[]{:S(2)}) copy-start(f32[5,2048]{1,0:T(8,128)} %param.11) | copy-start | bytes 122884
  7.2 184.4 %all-gather.4.cloned.1.call-start = ((), (), s32[]{:S(2)}) async-start(), calls=%async_computation | async-start | bytes 2228224 | tf_op jit(solution)/shard_map/all_gather | solution.py:38
  8.6 11.0 %collective-permute-start.1 = (bf16[1280,2]{1,0:T(8,128)(2,1)S(1)}, bf16[1280,2]{1,0:T(8,128)(2,1)S(1)}, u32[]{:S(2)}, u32[]{:S(2)}) collective-permute-start(bf16[1280,2]{1,0:T(8,128)(2,1)S(1)} %get-tuple-element.26), channel_id=1, source_target_pairs={{16,0},{32,16},{48,32},{64,48},{80,64},{96,80},{112,96},{128,112},... | collective-permute-start | bytes 15368 | tf_op jit(solution)/shard_map/ppermute | solution.py:18
  11.2 9.4 %slice-start.1 = ((s8[5242880]{0:T(1024)(128)(4,1)}), s8[4194304]{0:T(1024)(128)(4,1)S(1)}, s32[]{:S(2)}) async-start(s8[5242880]{0:T(1024)(128)(4,1)} %bitcast.52), calls=%async_computation.3 | async-start | bytes 8388608
  11.2 9.4 %collective-permute-start = (bf16[1280,2]{1,0:T(8,128)(2,1)S(1)}, bf16[1280,2]{1,0:T(8,128)(2,1)S(1)}, u32[]{:S(2)}, u32[]{:S(2)}) collective-permute-start(bf16[1280,2]{1,0:T(8,128)(2,1)S(1)} %get-tuple-element.27), channel_id=1, source_target_pairs={{0,16},{16,32},{32,48},{48,64},{64,80},{80,96},{96,112},{112,128},... | collective-permute-start | bytes 15368 | tf_op jit(solution)/shard_map/ppermute | solution.py:17
  20.5 17.9 %copy-start.3 = (s32[48,2]{0,1:T(2,128)S(1)}, s32[48,2]{0,1:T(2,128)}, u32[]{:S(2)}) copy-start(s32[48,2]{0,1:T(2,128)} %param.12) | copy-start | bytes 1156
  29.4 2.4 copy-start.1
  32.1 39.4 %collective-permute-start.2 = (bf16[384,2048]{1,0:T(8,128)(2,1)S(1)}, bf16[384,2048]{1,0:T(8,128)(2,1)}, u32[]{:S(2)}, u32[]{:S(2)}) collective-permute-start(bf16[384,2048]{1,0:T(8,128)(2,1)S(1)} %get-tuple-element.24), channel_id=1, source_target_pairs={{0,1},{1,2},{2,3},{3,4},{4,5},{5,6},{6,7},{7,8},{8,9},{9,10},{10,1... | collective-permute-start | bytes 4718600 | tf_op jit(solution)/shard_map/ppermute | solution.py:17
  36.8 40.5 %collective-permute-start.3 = (bf16[384,2048]{1,0:T(8,128)(2,1)S(1)}, bf16[384,2048]{1,0:T(8,128)(2,1)}, u32[]{:S(2)}, u32[]{:S(2)}) collective-permute-start(bf16[384,2048]{1,0:T(8,128)(2,1)S(1)} %get-tuple-element.25), channel_id=1, source_target_pairs={{1,0},{2,1},{3,2},{4,3},{5,4},{6,5},{7,6},{8,7},{9,8},{10,9},{11,1... | collective-permute-start | bytes 4718600 | tf_op jit(solution)/shard_map/ppermute | solution.py:18
  38.2 378.1 %all-gather.6.cloned.1.call-start = ((), (), s32[]{:S(2)}) async-start(), calls=%async_computation.1 | async-start | bytes 53477376 | tf_op jit(solution)/shard_map/all_gather | solution.py:62
Sparse Core Ops, SparseCore 0:
  38.3 102.5 all-gather.3
  161.3 254.9 all-gather.5
